TPU v7x, 32 devices: a whole 2x2x4 slice. The times are simulated.
32 devices in a mesh: groups: 2 (over x), tile: 16 (over z, y, core).
Axes of the slice: x: 2, y: 2, z: 4, core: 2. Of those that a mesh axis runs over, the one named last changes fastest.
Arguments:
- bands: bfloat16 [6144, 1312], P(('groups', 'tile')), parts along dimension 0, may hold values from -6 to 6
- send_table: int32 [16, 384], P('tile'), may hold values from 0 to 191, as said below
- recv_table: int32 [4, 3072], P(None, 'tile'), may hold values from 0 to 383, as said below
- regrid_weight: bfloat16 [3072, 1024], P('tile'), may hold values from 0.0049743652 to 0.25
- embed_weight: bfloat16 [1312, 384], replicated, may hold values from -0.15625 to 0.15625
- norm1_gain: float32 [2, 384], replicated, may hold values from 0.5 to 1.5
- qkv_weight: bfloat16 [2, 384, 1152], replicated, may hold values from -0.3125 to 0.3125
- rel_bias: float32 [2, 12, 225], replicated, may hold values from -6 to 400
- proj_weight: bfloat16 [2, 384, 384], replicated, may hold values from -0.3125 to 0.3125
- norm2_gain: float32 [2, 384], replicated, may hold values from 0.5 to 1.5
- up_weight: bfloat16 [2, 384, 1536], replicated, may hold values from -0.3125 to 0.3125
- down_weight: bfloat16 [2, 1536, 384], replicated, may hold values from -0.15625 to 0.15625
- unembed_weight: bfloat16 [384, 1312], replicated, may hold values from -0.3125 to 0.3125
Outputs:
- increment: float32 [6144, 1312], P(('groups', 'tile')), parts along dimension 0
There are 2 independent parts, one for each index of `groups`. A program takes and returns all parts, laid end to end along the dimension named above; an argument that names none is the same for every part. Nothing has to cross between parts.
Inputs may be any that keep to these rules, and one draw needn't show every extreme that they name: `send_table`: row s lists 24 local block indices of device s for each receiving device in order; every local block appears exactly twice in a row. `recv_table`: slot s * 24 + c of a device is the c-th block that device s passes to it; for each l, rows 2 * l and 2 * l + 1 of a device's patches together name each of its 384 slots exactly once.
All inputs are finite; a program needn't handle non-finite values.
Results may differ from a plain program's by a relative error of at most 0.018.
Values may be sent and summed in bfloat16 or wider, within the bound.
No kernel may reach another device: no remote copies, remote signals or barrier semaphores. Data moves between devices by JAX's collectives and lax.ppermute only.
A program may use at most 128 MiB of HBM per device.

v0:
```python
import jax
import jax.numpy as jnp
import numpy as np
from jax import lax
from jax.sharding import PartitionSpec as P

D = 384
CH = 82
PIX = 16
WIN = 8
K = 4
BLOCKS = 2
ROWS = 24
PD = 192


norm_eps = 1e-05


def from_behind(value, axis, steps):
    count = lax.axis_size(axis)
    pairs = [(source, (source + steps) % count) for source in range(count)]
    return lax.ppermute(value, axis, pairs)


def offset_onehot(window_side):
    coords = np.arange(window_side * window_side)
    row_pos = coords // window_side
    col_pos = coords % window_side
    span = 2 * window_side - 1
    offset_index = (row_pos[:, None] - row_pos[None, :] + window_side - 1) * span + (
        col_pos[:, None] - col_pos[None, :] + window_side - 1
    )
    return (offset_index.reshape(-1)[:, None] == np.arange(span * span)[None, :]).astype(np.float32)


def window_bias(bias_rows):
    lookup = jnp.asarray(offset_onehot(WIN).T)
    flat_bias = jnp.dot(bias_rows, lookup, precision=lax.Precision.HIGHEST)
    return flat_bias.reshape(bias_rows.shape[0], WIN * WIN, WIN * WIN)


def layer_norm(values, gain_vector):
    average = jnp.mean(values, axis=-1, keepdims=True)
    centred = values - average
    spread = jnp.mean(centred * centred, axis=-1, keepdims=True)
    return centred * lax.rsqrt(spread + norm_eps) * gain_vector


def attend(token_grid, gain_vector, qkv_block, proj_block, bias_table, shifted):
    grid_rows, grid_cols, width = token_grid.shape
    head_count = bias_table.shape[0]
    head_size = width // head_count
    shift_by = WIN // 2
    if shifted:
        rolled = jnp.roll(token_grid, -shift_by, axis=0).astype(jnp.float32)
    else:
        rolled = token_grid.astype(jnp.float32)
    normed = layer_norm(rolled, gain_vector).astype(jnp.bfloat16)
    window_rows = grid_rows // WIN
    window_cols = grid_cols // WIN
    window_count = window_rows * window_cols
    windows = (
        normed.reshape(window_rows, WIN, window_cols, WIN, width)
        .transpose(0, 2, 1, 3, 4)
        .reshape(window_count * WIN * WIN, width)
    )
    packed = jnp.dot(windows, qkv_block, preferred_element_type=jnp.float32).astype(jnp.bfloat16)
    packed = packed.reshape(window_count, WIN * WIN, 3, head_count, head_size)
    query_rows = packed[:, :, 0]
    key_rows = packed[:, :, 1]
    value_rows = packed[:, :, 2]
    scores = (
        jnp.einsum("wihd,wjhd->whij", query_rows, key_rows, preferred_element_type=jnp.float32)
        * head_size ** (-0.5)
        + bias_table[None]
    )
    if shifted:
        last_row = jnp.arange(window_count) // window_cols == window_rows - 1
        upper_half = jnp.arange(WIN * WIN) // WIN >= shift_by
        same_side = upper_half[:, None] == upper_half[None, :]
        allowed = jnp.logical_or(
            jnp.logical_not(last_row)[:, None, None, None], same_side[None, None]
        )
        scores = jnp.where(allowed, scores, -1e30)
    row_max = jnp.max(scores, axis=-1, keepdims=True)
    weights_exp = jnp.exp(scores - row_max)
    probs = (weights_exp / jnp.sum(weights_exp, axis=-1, keepdims=True)).astype(jnp.bfloat16)
    mixed_heads = jnp.einsum(
        "whij,wjhd->wihd", probs, value_rows, preferred_element_type=jnp.float32
    ).astype(jnp.bfloat16)
    mixed_heads = mixed_heads.reshape(window_count * WIN * WIN, width)
    result = jnp.dot(mixed_heads, proj_block, preferred_element_type=jnp.float32).astype(
        jnp.bfloat16
    )
    result = (
        result.reshape(window_rows, window_cols, WIN, WIN, width)
        .transpose(0, 2, 1, 3, 4)
        .reshape(grid_rows, grid_cols, width)
    )
    if shifted:
        return jnp.roll(result, shift_by, axis=0)
    return result


def swin_update(state, attended, gain_vector, up_block, down_block):
    residual = state.astype(jnp.float32) + attended.astype(jnp.float32)
    normed = layer_norm(residual, gain_vector).astype(jnp.bfloat16)
    hidden = jax.nn.gelu(jnp.dot(normed, up_block, preferred_element_type=jnp.float32)).astype(
        jnp.bfloat16
    )
    return (residual + jnp.dot(hidden, down_block, preferred_element_type=jnp.float32)).astype(
        jnp.bfloat16
    )


def body(
    bands,
    send_table,
    recv_table,
    regrid_weight,
    embed_weight,
    norm1_gain,
    qkv_weight,
    rel_bias,
    proj_weight,
    norm2_gain,
    up_weight,
    down_weight,
    unembed_weight,
):
    outgoing = bands[send_table[0]]
    incoming = lax.all_to_all(outgoing, "tile", split_axis=0, concat_axis=0, tiled=True)
    picked = incoming[recv_table].reshape(K, PD, PIX, CH)
    mixing = regrid_weight.reshape(PD, K, PIX, PIX)
    pixels = (
        jnp.einsum("pkij,kpjc->pic", mixing, picked, preferred_element_type=jnp.float32)
        .astype(jnp.bfloat16)
        .reshape(PD, PIX * CH)
    )
    state = jnp.dot(pixels, embed_weight, preferred_element_type=jnp.float32).astype(jnp.bfloat16)
    half_width = WIN // 2
    for block_index in range(BLOCKS):
        bias_table = window_bias(rel_bias[block_index])
        token_grid = state.reshape(ROWS, WIN, D)
        gain_one = norm1_gain[block_index]
        qkv_block = qkv_weight[block_index]
        proj_block = proj_weight[block_index]
        if block_index % 2 == 0:
            attended = attend(token_grid, gain_one, qkv_block, proj_block, bias_table, False)
        else:
            right_strip = from_behind(token_grid[:, :half_width], "tile", -1)
            framed = jnp.concatenate([token_grid[:, half_width:], right_strip], axis=1)
            result = attend(framed, gain_one, qkv_block, proj_block, bias_table, True)
            left_part = from_behind(result[:, half_width:], "tile", 1)
            attended = jnp.concatenate([left_part, result[:, :half_width]], axis=1)
        state = swin_update(
            state,
            attended.reshape(PD, D),
            norm2_gain[block_index],
            up_weight[block_index],
            down_weight[block_index],
        )
    out_pixels = jnp.dot(state, unembed_weight, preferred_element_type=jnp.float32).astype(
        jnp.bfloat16
    )
    contribution = jnp.einsum(
        "pkij,pic->kpjc",
        mixing,
        out_pixels.reshape(PD, PIX, CH),
        preferred_element_type=jnp.float32,
    )
    contribution = contribution.reshape(K * PD, PIX * CH)
    slot_sums = (
        jnp.zeros((outgoing.shape[0], PIX * CH), jnp.float32)
        .at[recv_table.reshape(-1)]
        .add(contribution)
    )
    returned = lax.all_to_all(
        slot_sums.astype(jnp.bfloat16), "tile", split_axis=0, concat_axis=0, tiled=True
    )
    return (
        jnp.zeros((PD, PIX * CH), jnp.float32).at[send_table[0]].add(returned.astype(jnp.float32))
    )


def solution(mesh):
    in_specs = (
        P(("groups", "tile"), None),
        P("tile", None),
        P(None, "tile"),
        P("tile", None),
        P(),
        P(),
        P(),
        P(),
        P(),
        P(),
        P(),
        P(),
        P(),
    )
    out_specs = P(("groups", "tile"), None)
    return jax.shard_map(body, mesh=mesh, in_specs=in_specs, out_specs=out_specs, check_vma=False)
```

profile of v0, /device:TPU:0, one launch (start us, length us, event | category | flops | bytes accessed | tf_op | source)
XLA Modules:
  0.0 157.7 jit_solution(6629909322178204840)
XLA Ops:
  0.0 0.8 fusion.132
  0.8 5.1 %gather_fusion = bf16[384,1312]{1,0:T(8,128)(2,1)} fusion(bf16[192,1312]{1,0:T(8,128)(2,1)} %param.15, s32[1024]{0:T(1024)S(1)} %pad_clamp_fusion.1), kind=kCustom, calls=%fused_computation | custom fusion | bytes 2016768 | tf_op jit(solution)/shard_map/gather | solution.py:132
  5.9 7.5 %all-to-all-start = ((bf16[16,24,1312]{2,1,0:T(8,128)(2,1)}), bf16[16,24,1312]{2,1,0:T(8,128)(2,1)S(1)}, u32[]{:S(2)}, u32[]{:S(2)}) async-start(bf16[16,24,1312]{2,1,0:T(8,128)(2,1)} %bitcast.1), calls=%async_computation | async-start | bytes 2162688 | tf_op jit(solution)/shard_map/all_to_all | solution.py:133
  13.8 4.0 %copy.72 = bf16[192,4,16,16]{2,3,1,0:T(8,128)(2,1)} copy(bf16[192,4,16,16]{0,3,2,1:T(8,128)(2,1)S(1)} %bitcast.171) | data formatting | bytes 786432 | tf_op jit(solution)/shard_map/reshape | solution.py:135
  17.8 6.7 %convolution_bitcast_fusion.1 = f32[12,64,64]{2,0,1:T(8,128)S(1)} fusion(f32[64,64,225]{2,1,0:T(8,128)} %constant.80, f32[1,12,225]{2,0,1:T(1,128)S(1)} %get-tuple-element.18), kind=kOutput, calls=%fused_computation.27 | convolution fusion | flops 132710400 | bytes 3893808 | tf_op jit(solution)/shard_map/dot_general | solution.py:39
  25.0 8.0 %convolution_bitcast_fusion = f32[12,64,64]{2,0,1:T(8,128)} fusion(f32[64,64,225]{2,1,0:T(8,128)} %constant.80, f32[1,12,225]{2,0,1:T(1,128)S(1)} %get-tuple-element.17), kind=kOutput, calls=%fused_computation.26 | convolution fusion | flops 132710400 | bytes 3893808 | tf_op jit(solution)/shard_map/dot_general | solution.py:39
  33.0 3.9 %all-to-all-done = bf16[16,24,1312]{2,1,0:T(8,128)(2,1)S(1)} async-done(((bf16[16,24,1312]{2,1,0:T(8,128)(2,1)}), bf16[16,24,1312]{2,1,0:T(8,128)(2,1)S(1)}, u32[]{:S(2)}, u32[]{:S(2)}) %all-to-all-start) | async-done | bytes 1007648 | tf_op jit(solution)/shard_map/all_to_all | solution.py:133
  36.9 3.8 %gather_fusion.1 = bf16[768,1312]{1,0:T(8,128)(2,1)} fusion(bf16[384,1312]{1,0:T(8,128)(2,1)S(1)} %bitcast.166, s32[1024]{0:T(1024)S(1)} %pad_clamp_fusion), kind=kCustom, calls=%fused_computation.1 | custom fusion | bytes 4033536 | tf_op jit(solution)/shard_map/gather | solution.py:134
  40.7 8.2 %reshape.382 = bf16[4,192,16,82]{3,2,1,0:T(8,128)(2,1)} reshape(bf16[768,1312]{1,0:T(8,128)(2,1)} %gather_fusion.1) | data formatting | bytes 4030464 | tf_op jit(solution)/shard_map/reshape | solution.py:134
  48.9 3.8 %fusion.15 = bf16[192,16,82]{2,1,0:T(8,128)(2,1)S(1)} fusion(bf16[192,4,16,16]{2,3,1,0:T(8,128)(2,1)} %copy.72, bf16[4,192,16,82]{3,2,1,0:T(8,128)(2,1)} %reshape.382), kind=kOutput, calls=%fused_computation.25 | convolution fusion | flops 32495616 | bytes 2912256 | tf_op jit(solution)/shard_map/pkij,kpjc->pic/dot_general | solution.py:137
  52.7 1.0 reshape.330
  53.6 1.9 %fusion.154 = (f32[192]{0:T(256)S(1)}, f32[192,384]{1,0:T(8,128)S(1)}) fusion(bf16[192,1312]{1,0:T(8,128)(2,1)S(1)} %reshape.330, bf16[1312,384]{1,0:T(8,128)(2,1)} %param.19), kind=kOutput, calls=%fused_computation.184 | convolution fusion | flops 193683264 | bytes 1807104 | tf_op jit(solution)/shard_map/dot_general | solution.py:141
  55.7 0.5 convolution_convert_fusion.2
  56.2 0.3 copy.56
  56.5 0.5 reshape.331
  57.0 1.4 fusion.151
  58.4 0.7 copy-done.3
  59.1 0.4 fusion.12
  59.5 1.6 %fusion.155 = f32[3,12,64]{2,1,0:T(8,128)S(1)} fusion(f32[12,64,64]{1,2,0:T(8,128)S(1)} %copy.61, bf16[3,64,1,12,32]{1,0,4,3,2:T(4,128)(2,1)} %copy-done.3, bf16[3,64,1,12,32]{1,0,4,3,2:T(4,128)(2,1)S(1)} %get-tuple-element.13), kind=kOutput, calls=%fused_computation.185 | convolution fusion | flops 10027071 | bytes 500736 | tf_op jit(solution)/shard_map/sub | solution.py:87
  61.1 1.4 fusion.56
  62.6 0.3 copy.63
  62.8 0.3 reshape.333
  63.1 0.5 copy-done.5
  63.6 0.4 fusion.156
  64.3 2.6 %fusion.75 = bf16[192,384]{1,0:T(8,128)(2,1)S(1)} fusion(f32[192,384]{1,0:T(8,128)S(1)} %get-tuple-element.22, bf16[2,1536,384]{2,1,0:T(8,128)(2,1)} %param.26, bf16[2,384,1536]{2,1,0:T(8,128)(2,1)} %param.25, f32[384]{0:T(512)S(1)} %get-tuple-element.8, f32[192]{0:T(256)S(1)} %add_rsqrt_fusion.2, f32[192]{0:T(256)S(1)} %broadcast_multiply_fusion.2), kind=kOutput, calls=%fused_computation.69 | convolution fusion | flops 456081408 | bytes 3100672 | tf_op jit(solution)/shard_map/dot_general | solution.py:112
  66.9 5.6 %collective-permute-start = (bf16[24,4,384]{2,1,0:T(4,128)(2,1)S(1)}, bf16[24,4,384]{2,1,0:T(4,128)(2,1)S(1)}, u32[]{:S(2)}, u32[]{:S(2)}) collective-permute-start(bf16[24,4,384]{2,1,0:T(4,128)(2,1)S(1)} %get-tuple-element.16), channel_id=1, source_target_pairs={{0,15},{1,0},{2,1},{3,2},{4,3},{5,4},{6,5},{7,6},{8,7},{9,8},{10,9... | collective-permute-start | bytes 221192 | tf_op jit(solution)/shard_map/ppermute | solution.py:23
  73.0 1.6 %collective-permute-done = bf16[24,4,384]{2,1,0:T(4,128)(2,1)S(1)} collective-permute-done((bf16[24,4,384]{2,1,0:T(4,128)(2,1)S(1)}, bf16[24,4,384]{2,1,0:T(4,128)(2,1)S(1)}, u32[]{:S(2)}, u32[]{:S(2)}) %collective-permute-start) | collective-permute-done | bytes 73760 | tf_op jit(solution)/shard_map/ppermute | solution.py:23
  74.9 1.6 %convolution_convert_fusion.1 = bf16[192,1152]{1,0:T(8,128)(2,1)S(1)} fusion(bf16[2,384,1152]{2,1,0:T(8,128)(2,1)} %param.21, f32[384]{0:T(512)S(1)} %get-tuple-element.5, f32[24,8]{1,0:T(8,128)S(1)} %add_rsqrt_fusion, f32[24,8]{1,0:T(8,128)S(1)} %broadcast_multiply_fusion, bf16[24,4,384]{2,1,0:T(4,128)(2,1)S(1)} %collective-permute-done, ...), kind=kOutput, calls=%fused_computation.9 | convolution fusion | flops 170827776 | bytes 1600512 | tf_op jit(solution)/shard_map/dot_general | solution.py:68
  76.8 0.4 reshape.335
  77.2 1.4 fusion.150
  78.6 0.7 copy-done.2
  79.3 0.4 fusion.11
  79.7 1.7 %fusion.157 = f32[3,12,64]{2,1,0:T(8,128)S(1)} fusion(f32[12,64,64]{1,2,0:T(8,128)S(1)} %copy.69, pred[3,64,64]{1,2,0:T(8,128)(4,1)S(1)} %broadcast_or_fusion, bf16[3,64,1,12,32]{1,0,4,3,2:T(4,128)(2,1)} %copy-done.2, bf16[3,64,1,12,32]{1,0,4,3,2:T(4,128)(2,1)S(1)} %get-tuple-element.10), kind=kOutput, calls=%fused_computation.187 | convolution fusion | flops 10174527 | bytes 513024 | tf_op jit(solution)/shard_map/sub | solution.py:87
  81.4 1.4 fusion.57
  82.8 0.3 copy.71
  83.1 0.3 reshape.337
  83.3 0.5 copy-done.6
  83.9 0.3 convolution_convert_fusion.5
  84.4 6.5 %collective-permute-done.1 = bf16[24,4,384]{2,1,0:T(4,128)(2,1)S(1)} collective-permute-done((bf16[24,4,384]{2,1,0:T(4,128)(2,1)S(1)}, bf16[24,4,384]{2,1,0:T(4,128)(2,1)S(1)}, u32[]{:S(2)}, u32[]{:S(2)}) %collective-permute-start.1) | collective-permute-done | bytes 73760 | tf_op jit(solution)/shard_map/ppermute | solution.py:23
  91.3 2.6 %fusion.70 = bf16[192,384]{1,0:T(8,128)(2,1)S(1)} fusion(bf16[2,1536,384]{2,1,0:T(8,128)(2,1)} %param.26, bf16[2,384,1536]{2,1,0:T(8,128)(2,1)} %param.25, bf16[192,384]{1,0:T(8,128)(2,1)S(1)} %fusion.75, f32[384]{0:T(512)S(1)} %get-tuple-element.7, f32[192]{0:T(256)S(1)} %add_rsqrt_fusion.1, f32[192]{0:T(256)S(1)} %broadcast_multiply_fusion.1, ...), kind=kOutput, calls=%fused_computation.68 | convolution fusion | flops 457408512 | bytes 3248128 | tf_op jit(solution)/shard_map/dot_general | solution.py:112
  93.8 0.5 convolution_convert_fusion
  94.4 1.5 reshape.338
  95.9 2.8 %fusion.158 = f32[192,82,64]{1,2,0:S(1)} fusion(bf16[192,16,82]{2,1,0:T(8,128)(2,1)S(1)} %reshape.338, bf16[192,16,64]{1,2,0:T(8,128)(2,1)} %bitcast.167), kind=kOutput, calls=%fused_computation.188 | convolution fusion | flops 32243712 | bytes 4927488
  98.7 3.3 %copy.80 = f32[4,192,16,82]{3,2,1,0:T(8,128)} copy(f32[4,192,16,82]{3,2,0,1:T(8,128)S(1)} %bitcast.168) | data formatting | bytes 8060928 | tf_op jit(solution)/shard_map/reshape | solution.py:173
  102.0 7.5 %reshape.383 = f32[768,1312]{1,0:T(8,128)} reshape(f32[4,192,16,82]{3,2,1,0:T(8,128)} %copy.80) | data formatting | bytes 8060928 | tf_op jit(solution)/shard_map/reshape | solution.py:173
  109.5 12.1 %scatter_custom_fusion = f32[384,1312]{1,0:T(8,128)S(1)} fusion(s32[768]{0:T(1024)S(1)} %fusion.131, f32[768,1312]{1,0:T(8,128)} %reshape.383, f32[]{:T(128)} %constant.58.clone.1), kind=kCustom, calls=%fused_computation.72 | custom fusion | flops 1007616 | bytes 2015744 | tf_op jit(solution)/shard_map/scatter-add | solution.py:177
  121.8 30.5 %all_to_all.21 = bf16[16,24,1312]{2,1,0:T(8,128)(2,1)S(1)} all-to-all(bf16[16,24,1312]{2,1,0:T(8,128)(2,1)S(1)} %bitcast.170), channel_id=1, replica_groups=mesh['groups'=2,'tile'=16] {'tile'}, dimensions={0} | all-to-all | bytes 2015232 | tf_op jit(solution)/shard_map/all_to_all | solution.py:179
  152.3 5.4 %scatter_custom_fusion.1 = f32[192,1312]{1,0:T(8,128)} fusion(s32[384]{0:T(512)S(1)} %fusion.132, bf16[384,1312]{1,0:T(8,128)(2,1)S(1)} %bitcast.169, f32[]{:T(128)} %constant.58.clone.1), kind=kCustom, calls=%fused_computation.11 | custom fusion | flops 1007616 | bytes 2088964 | tf_op jit(solution)/shard_map/scatter-add | solution.py:183
  (58 shorter events, 2.8 us)
Async XLA Ops:
  0.0 93.8 %copy-start = (bf16[384,1312]{0,1:T(8,128)(2,1)S(1)}, bf16[384,1312]{0,1:T(8,128)(2,1)}, u32[]{:S(2)}) copy-start(bf16[384,1312]{0,1:T(8,128)(2,1)} %param.27) | copy-start | bytes 3022852
  5.9 7.6 %copy-start.8 = (s32[4,192]{1,0:T(4,128)S(1)}, s32[4,192]{1,0:T(4,128)}, u32[]{:S(2)}) copy-start(s32[4,192]{1,0:T(4,128)} %param.17) | copy-start | bytes 9220
  5.9 7.7 %copy-start.4 = (bf16[192,1024]{1,0:T(8,128)(2,1)S(1)}, bf16[192,1024]{1,0:T(8,128)(2,1)}, u32[]{:S(2)}) copy-start(bf16[192,1024]{1,0:T(8,128)(2,1)} %param.18) | copy-start | bytes 1179652
  5.9 31.0 %all-to-all-start = ((bf16[16,24,1312]{2,1,0:T(8,128)(2,1)}), bf16[16,24,1312]{2,1,0:T(8,128)(2,1)S(1)}, u32[]{:S(2)}, u32[]{:S(2)}) async-start(bf16[16,24,1312]{2,1,0:T(8,128)(2,1)} %bitcast.1), calls=%async_computation | async-start | bytes 2162688 | tf_op jit(solution)/shard_map/all_to_all | solution.py:133
  13.8 4.0 %copy-start.7 = (f32[2,12,225]{2,0,1:T(2,128)S(1)}, f32[2,12,225]{2,0,1:T(2,128)}, u32[]{:S(2)}) copy-start(f32[2,12,225]{2,0,1:T(2,128)} %param.22) | copy-start | bytes 64804
  17.8 7.0 %copy-start.9 = (f32[2,384]{1,0:T(2,128)S(1)}, f32[2,384]{1,0:T(2,128)}, u32[]{:S(2)}) copy-start(f32[2,384]{1,0:T(2,128)} %param.20) | copy-start | bytes 9220
  17.8 7.1 %copy-start.10 = (f32[2,384]{1,0:T(2,128)S(1)}, f32[2,384]{1,0:T(2,128)}, u32[]{:S(2)}) copy-start(f32[2,384]{1,0:T(2,128)} %param.24) | copy-start | bytes 9220
  53.6 2.1 %copy-start.11 = (bf16[2,384,1152]{2,1,0:T(8,128)(2,1)S(1)}, bf16[2,384,1152]{2,1,0:T(8,128)(2,1)}, u32[]{:S(2)}) copy-start(bf16[2,384,1152]{2,1,0:T(8,128)(2,1)} %param.21) | copy-start | bytes 5308420
  58.4 0.7 copy-start.3
  62.6 1.1 copy-start.5
  64.2 8.5 %copy-start.1 = (f32[12,64,64]{2,0,1:T(8,128)S(1)}, f32[12,64,64]{2,0,1:T(8,128)}, u32[]{:S(2)}) copy-start(f32[12,64,64]{2,0,1:T(8,128)} %convolution_bitcast_fusion) | copy-start | bytes 589828
  66.9 7.6 %collective-permute-start = (bf16[24,4,384]{2,1,0:T(4,128)(2,1)S(1)}, bf16[24,4,384]{2,1,0:T(4,128)(2,1)S(1)}, u32[]{:S(2)}, u32[]{:S(2)}) collective-permute-start(bf16[24,4,384]{2,1,0:T(4,128)(2,1)S(1)} %get-tuple-element.16), channel_id=1, source_target_pairs={{0,15},{1,0},{2,1},{3,2},{4,3},{5,4},{6,5},{7,6},{8,7},{9,8},{10,9... | collective-permute-start | bytes 221192 | tf_op jit(solution)/shard_map/ppermute | solution.py:23
  78.6 0.7 copy-start.2
  82.8 1.1 copy-start.6
  84.3 6.6 %collective-permute-start.1 = (bf16[24,4,384]{2,1,0:T(4,128)(2,1)S(1)}, bf16[24,4,384]{2,1,0:T(4,128)(2,1)S(1)}, u32[]{:S(2)}, u32[]{:S(2)}) collective-permute-start(bf16[24,4,384]{2,1,0:T(4,128)(2,1)S(1)} %fusion.130), channel_id=1, source_target_pairs={{0,1},{1,2},{2,3},{3,4},{4,5},{5,6},{6,7},{7,8},{8,9},{9,10},{10,1... | collective-permute-start | bytes 221192 | tf_op jit(solution)/shard_map/ppermute | solution.py:23
where the time goes:
time: 159 us; the launch traced here: 158 us
  local copies, waits for them, and re-layouts  43 us (27%)
  matrix products  38.7 us (24%)
  blocking collectives  30.5 us (19%)
  other arithmetic  19.9 us (13%)
  starting transfers between devices  13.2 us (8%)
  waiting for transfers between devices  11.9 us (7%)
    all_to_all x1, blocking collectives, body(): lax.all_to_all(slot_sums.astype(jnp.bfloat16), 'tile', split_axis=0, conc...  30.5 us
    dot_general x2, matrix products, window_bias(): flat_bias = jnp.dot(bias_rows, lookup, precision=lax.Precision.HIGHEST)  14.8 us
    scatter-add x1, other arithmetic, body(): slot_sums = jnp.zeros((outgoing.shape[0], PIX * CH), jnp.float32).at[recv...  12.1 us
    reshape x2, local copies, waits for them, and re-layouts, body(): contribution = contribution.reshape(K * PD, PIX * CH)  10.8 us
    reshape x1, local copies, waits for them, and re-layouts, body(): picked = incoming[recv_table].reshape(K, PD, PIX, CH)  8.19 us
    ppermute x2, waiting for transfers between devices, from_behind(): return lax.ppermute(value, axis, pairs)  8.09 us
    all_to_all x1, starting transfers between devices, body(): lax.all_to_all(outgoing, 'tile', split_axis=0, concat_axis=0, tiled=True)  7.55 us
    ppermute x2, starting transfers between devices, from_behind(): return lax.ppermute(value, axis, pairs)  5.69 us
  transfers between devices with their start and end apart: 3, of which 3 were waited for; matrix products, arithmetic and copies ran while one was open for 13% of the time, Pallas kernels for 0%

commit v1 on v0

v1 whole, which is shorter than its diff:
```python
import jax
import jax.numpy as jnp
import numpy as np
from jax import lax
from jax.experimental import pallas as pl
from jax.experimental.pallas import tpu as pltpu
from jax.sharding import PartitionSpec as P

WIN = 8
ROWS = 24
K = 4
LANES = 128
GROUP = 8

norm_eps = 1e-05
F32 = jnp.float32
BF16 = jnp.bfloat16


def iota(shape, axis):
    return lax.broadcasted_iota(jnp.int32, shape, axis)


def mm(a, b):
    return jnp.dot(a, b, preferred_element_type=F32)


def mm_tn(a, b):
    return lax.dot_general(a, b, (((0,), (0,)), ((), ())), preferred_element_type=F32)


def mm_nt(a, b):
    return lax.dot_general(a, b, (((1,), (1,)), ((), ())), preferred_element_type=F32)


def full(x):
    return pl.BlockSpec(memory_space=pltpu.VMEM)


def call(kernel, outs, args, any_args=(), scratch=(), flops=0, name=None):
    in_specs = [pl.BlockSpec(memory_space=pltpu.VMEM)] * len(args)
    in_specs += [pl.BlockSpec(memory_space=pl.ANY)] * len(any_args)
    moved = sum(int(np.prod(a.shape)) * a.dtype.itemsize for a in [*args, *any_args, *outs])
    many = len(outs) > 1
    return pl.pallas_call(
        kernel,
        out_shape=tuple(outs) if many else outs[0],
        in_specs=in_specs,
        out_specs=tuple([full(o) for o in outs]) if many else full(outs[0]),
        scratch_shapes=list(scratch),
        compiler_params=pltpu.CompilerParams(vmem_limit_bytes=48 << 20),
        cost_estimate=pl.CostEstimate(flops=int(flops), bytes_accessed=moved, transcendentals=0),
        name=name,
    )(*args, *any_args)


def sds(shape, dtype):
    return jax.ShapeDtypeStruct(shape, dtype)


def pick_kernel(bands_ref, send_ref, out_ref):
    rows, slots = bands_ref.shape[0], send_ref.shape[1]
    onehot = (iota((rows, slots), 0) == send_ref[...]).astype(F32).astype(BF16)
    out_ref[...] = mm_tn(onehot, bands_ref[...]).astype(BF16)


def spread(weights, fixed_first, pix):
    rows = weights.shape[0]
    width = pix * GROUP
    shape = (pix * pix, pix * width)
    r, c = iota(shape, 0), iota(shape, 1)
    outer, inner = c // width, (c % width) // GROUP
    if fixed_first:
        sel = (r // pix == outer) & (r % pix == inner)
    else:
        sel = (r % pix == outer) & (r // pix == inner)
    out = mm(weights, sel.astype(F32).astype(BF16))
    own = iota(out.shape, 0) % GROUP == iota(out.shape, 1) % GROUP
    return jnp.where(own, out, 0.0)


def store_spread(out_ref, value, place, pix):
    groups = value.shape[0] // GROUP
    width = pix * GROUP
    for o in range(0, pix, 2):
        lo = value[:, o * width : (o + 1) * width].reshape(groups, GROUP, width)
        hi = value[:, (o + 1) * width : (o + 2) * width].reshape(groups, GROUP, width)
        both = jnp.concatenate([lo, hi], axis=1).astype(BF16)
        out_ref[:, o * GROUP : (o + 2) * GROUP, place * width : (place + 1) * width] = both


def prep_kernel(recv_col_ref, recv_ref, weight_ref, gather_ref, mix_ref, wsend_ref, select_ref):
    kk, pd = recv_ref.shape
    slots = 2 * pd
    pixsq = weight_ref.shape[1] // kk
    pix = int(round(pixsq**0.5))
    rows = kk * pd
    gather_ref[...] = (recv_col_ref[...] == iota((rows, slots), 1)).astype(F32).astype(BF16)
    r = iota((rows, pd), 0)
    slot = (r // (2 * GROUP)) * GROUP + r % GROUP
    level = (r // GROUP) % 2
    total = None
    chosen = None
    for k in range(kk):
        hit = (recv_ref[k : k + 1, :] == slot) & (level == k // 2)
        hit = hit.astype(F32)
        w_k = weight_ref[:, k * pixsq : (k + 1) * pixsq]
        term = mm(hit.astype(BF16), w_k)
        total = term if total is None else total + term
        chosen = hit if chosen is None else chosen + hit
        store_spread(mix_ref, spread(w_k, True, pix), k, pix)
    wsend_ref[...] = total.astype(BF16)
    select_ref[...] = chosen.astype(BF16)


def prep_back_kernel(weight_ref, mix_ref):
    rows, pixsq = weight_ref.shape
    pix = int(round(pixsq**0.5))
    groups = rows // (2 * GROUP)
    w3 = weight_ref[...].astype(F32).reshape(groups, 2, GROUP, pixsq)
    for level in range(2):
        w_l = w3[:, level].reshape(groups * GROUP, pixsq).astype(BF16)
        store_spread(mix_ref, spread(w_l, False, pix), level, pix)


def layer_norm(values, gain):
    average = jnp.mean(values, axis=-1, keepdims=True)
    centred = values - average
    spread_ = jnp.mean(centred * centred, axis=-1, keepdims=True)
    return centred * lax.rsqrt(spread_ + norm_eps) * gain


def softmax_parts(scores, side):
    out = []
    for m in range(scores.shape[1] // LANES):
        part = scores[:, m * LANES : (m + 1) * LANES]
        low = iota(part.shape, 1) % LANES < side
        top_lo = jnp.max(jnp.where(low, part, -3e38), axis=-1, keepdims=True)
        top_hi = jnp.max(jnp.where(low, -3e38, part), axis=-1, keepdims=True)
        out.append(jnp.exp(part - jnp.where(low, top_lo, top_hi)))
    return jnp.concatenate(out, axis=1)


def attend_rows(query, key, value, bias, heads, blocked):
    m, d = query.shape
    size = d // heads
    span = key.shape[0]
    head_of = iota((heads * span, d), 0) // span == iota((heads * span, d), 1) // size
    mask = head_of.astype(F32).astype(BF16)
    key_all = jnp.concatenate([key] * heads, axis=0) * mask
    value_all = jnp.concatenate([value] * heads, axis=0) * mask
    scores = mm_nt(query, key_all) * size ** (-0.5) + bias
    if blocked is not None:
        scores = jnp.where(blocked, -1e30, scores)
    weights = softmax_parts(scores, span)
    weights16 = weights.astype(BF16)
    total = mm(weights16, mask)
    return (mm(weights16, value_all) / total).astype(BF16)


def feed_forward(residual, gain2, up, down):
    normed = layer_norm(residual, gain2).astype(BF16)
    hidden = jax.nn.gelu(mm(normed, up)).astype(BF16)
    return (residual + mm(hidden, down)).astype(BF16)


def start(copies):
    for c in copies:
        c.start()
    return copies


def to_vmem(pairs, sem):
    return [pltpu.make_async_copy(a, b, sem.at[i]) for i, (a, b) in enumerate(pairs)]


def lay_tiles(rows, count):
    return jnp.concatenate([rows[:, t * LANES : (t + 1) * LANES] for t in range(count)], axis=0)


def first_kernel(
    inc_ref, gather_ref, gain1_ref, gain2_ref, bias_ref,
    mix_any, embed_any, qkv_any, proj_any, up_any, down_any,
    low_ref, high_ref,
    x_ref, p_ref, pix_ref, mix_ref, embed_ref, qkv_ref, proj_ref, up_ref, down_ref, sem,
):
    copies = start(to_vmem(
        [(mix_any, mix_ref), (embed_any, embed_ref), (qkv_any, qkv_ref), (proj_any, proj_ref),
         (up_any, up_ref), (down_any, down_ref)], sem))
    slots, width = inc_ref.shape
    pix = pix_ref.shape[1] // LANES
    ch = width // pix
    pd, d = embed_ref.shape[1] and pix_ref.shape[0], embed_ref.shape[1]
    kk = p_ref.shape[0]
    groups = pd // GROUP
    heads = bias_ref.shape[1] // (WIN * WIN)
    for j in range(pix):
        lo = (ch * j // LANES) * LANES
        hi = min(lo + 2 * LANES, width)
        off = ch * j - lo
        shape = (hi - lo, LANES)
        move = (iota(shape, 0) - off == iota(shape, 1)) & (iota(shape, 1) < ch)
        move = move.astype(F32).astype(BF16)
        x_ref[:, j * LANES : (j + 1) * LANES] = mm(inc_ref[:, lo:hi], move).astype(BF16)
    for j in range(0, pix, 2):
        cols = slice(j * LANES, (j + 2) * LANES)
        got = mm(gather_ref[...], x_ref[:, cols])
        for k in range(kk):
            p_ref[k, :, cols] = got[k * pd : (k + 1) * pd]
    copies[0].wait()

    def mix_group(g, carry):
        at = pl.ds(pl.multiple_of(g * GROUP, GROUP), GROUP)
        data = jnp.concatenate([lay_tiles(p_ref[k, at, :], pix) for k in range(kk)], axis=0)
        out = mm(mix_ref[g], data.astype(BF16))
        for i in range(pix):
            pix_ref[at, i * LANES : (i + 1) * LANES] = out[i * GROUP : (i + 1) * GROUP]
        return carry

    lax.fori_loop(0, groups, mix_group, 0, unroll=4)
    copies[1].wait()
    state = mm(pix_ref[...].astype(BF16), embed_ref[...]).astype(BF16).astype(F32)
    normed = layer_norm(state, gain1_ref[...]).astype(BF16)
    copies[2].wait()
    packed = mm(normed, qkv_ref[...]).astype(BF16)
    query, key, value = packed[:, :d], packed[:, d : 2 * d], packed[:, 2 * d :]
    half = pd // 2
    win_rows = ROWS // WIN
    part = half // win_rows
    mixed = [None] * (2 * win_rows)
    for w in range(win_rows):
        def rows(v):
            return jnp.concatenate(
                [v[w * part : (w + 1) * part], v[half + w * part : half + (w + 1) * part]], axis=0)
        out = attend_rows(rows(query), rows(key), rows(value), bias_ref[...], heads, None)
        mixed[w] = out[:part]
        mixed[win_rows + w] = out[part:]
    mixed = jnp.concatenate(mixed, axis=0)
    copies[3].wait()
    attended = mm(mixed, proj_ref[...]).astype(BF16)
    residual = state + attended.astype(F32)
    copies[4].wait()
    copies[5].wait()
    new = feed_forward(residual, gain2_ref[...], up_ref[...], down_ref[...])
    low_ref[...] = new[:half]
    high_ref[...] = new[half:]


def second_kernel(
    low_ref, high_ref, left_ref, right_ref, gain1_ref, gain2_ref, bias_ref,
    select_any, qkv_any, proj_any, up_any, down_any,
    out_ref,
    select_ref, qkv_ref, proj_ref, up_ref, down_ref, sem,
):
    copies = start(to_vmem(
        [(qkv_any, qkv_ref), (proj_any, proj_ref), (up_any, up_ref), (down_any, down_ref),
         (select_any, select_ref)], sem))
    half, d = low_ref.shape
    heads = bias_ref.shape[1] // (WIN * WIN)
    shift = half * (WIN // 2) // ROWS
    turn = lambda v: jnp.concatenate([v[shift:], v[:shift]], axis=0)
    back = lambda v: jnp.concatenate([v[half - shift :], v[: half - shift]], axis=0)
    own = jnp.concatenate([turn(low_ref[...]), turn(high_ref[...])], axis=0).astype(F32)
    strips = jnp.concatenate([turn(left_ref[...]), turn(right_ref[...])], axis=0).astype(F32)
    gain1 = gain1_ref[...]
    normed = layer_norm(own, gain1).astype(BF16)
    normed_s = layer_norm(strips, gain1).astype(BF16)
    copies[0].wait()
    packed = mm(normed, qkv_ref[...]).astype(BF16)
    packed_s = mm(normed_s, qkv_ref[:, d:]).astype(BF16)
    query, key, value = packed[:, :d], packed[:, d : 2 * d], packed[:, 2 * d :]
    key_s, value_s = packed_s[:, :d], packed_s[:, d:]
    win_rows = ROWS // WIN
    part = half // win_rows
    bias = bias_ref[...]
    span = WIN * WIN
    outs = [[], []]
    for w in range(win_rows):
        near = slice(w * part, (w + 1) * part)
        far = slice(half + w * part, half + (w + 1) * part)
        for side in range(2):
            if side == 0:
                q = query[near]
                k = jnp.concatenate([key_s[near], key[near]], axis=0)
                v = jnp.concatenate([value_s[near], value[near]], axis=0)
                b = bias[part:]
            else:
                q = query[far]
                k = jnp.concatenate([key[far], key_s[far]], axis=0)
                v = jnp.concatenate([value[far], value_s[far]], axis=0)
                b = bias[:part]
            blocked = None
            if w == win_rows - 1:
                shape = (part, heads * span)
                q_up = iota(shape, 0) % part >= part // 2
                k_up = iota(shape, 1) % part >= part // 2
                blocked = q_up != k_up
            outs[side].append(attend_rows(q, k, v, b, heads, blocked))
    mixed = jnp.concatenate(outs[0] + outs[1], axis=0)
    copies[1].wait()
    attended = mm(mixed, proj_ref[...]).astype(BF16)
    residual = own + attended.astype(F32)
    copies[2].wait()
    copies[3].wait()
    new = feed_forward(residual, gain2_ref[...], up_ref[...], down_ref[...])
    state = jnp.concatenate([back(new[:half]), back(new[half:])], axis=0)
    copies[4].wait()
    out_ref[...] = mm(select_ref[...], state).astype(BF16)


def last_kernel(state_ref, send_ref, unembed_ref, mix_any, out_ref, p_ref, slot_ref, mix_ref, sem):
    copy = pltpu.make_async_copy(mix_any, mix_ref, sem.at[0])
    copy.start()
    rows, d = state_ref.shape
    width = unembed_ref.shape[1]
    pix = width // LANES
    pd, total = out_ref.shape
    ch = total // pix
    groups = rows // (2 * GROUP)
    for j in range(0, pix, 2):
        cols = slice(j * LANES, (j + 2) * LANES)
        p_ref[:, cols] = mm(state_ref[...], unembed_ref[:, cols])
    copy.wait()

    def mix_group(g, carry):
        at = pl.ds(pl.multiple_of(g * 2 * GROUP, 2 * GROUP), 2 * GROUP)
        got = p_ref[at, :]
        data = jnp.concatenate([lay_tiles(got[:GROUP], pix), lay_tiles(got[GROUP:], pix)], axis=0)
        out = mm(mix_ref[g], data.astype(BF16))
        to = pl.ds(pl.multiple_of(g * GROUP, GROUP), GROUP)
        for i in range(pix):
            slot_ref[to, i * LANES : (i + 1) * LANES] = out[i * GROUP : (i + 1) * GROUP]
        return carry

    lax.fori_loop(0, groups, mix_group, 0, unroll=4)
    onehot = (iota((pd, send_ref.shape[1]), 0) == send_ref[...]).astype(F32).astype(BF16)
    tiles = [None] * (-(-total // LANES))
    for j in range(0, pix, 2):
        both = mm(onehot, slot_ref[:, j * LANES : (j + 2) * LANES].astype(BF16))
        for jj in (j, j + 1):
            val = both[:, (jj - j) * LANES : (jj - j + 1) * LANES]
            t, off = divmod(ch * jj, LANES)
            if off:
                val = pltpu.roll(val, off, 1)
            lane = iota(val.shape, 1)
            for tt, piece in ((t, jnp.where(lane >= off, val, 0.0)), (t + 1, jnp.where(lane < off, val, 0.0))):
                if tt == t + 1 and off + ch <= LANES:
                    continue
                tiles[tt] = piece if tiles[tt] is None else tiles[tt] + piece
    for t, tile in enumerate(tiles):
        hi = min((t + 1) * LANES, total)
        out_ref[:, t * LANES : hi] = tile[:, : hi - t * LANES]


def swap(value, axis):
    return lax.all_to_all(value, axis, split_axis=0, concat_axis=0, tiled=True)


def swap_pairs(value, axis):
    count = lax.axis_size(axis)
    rows, width = value.shape
    cap = rows // (2 * count)
    if cap % GROUP == 0:
        return swap(value, axis)
    groups = rows // (2 * GROUP)
    v = value.reshape(groups, 2, GROUP, width).transpose(1, 0, 2, 3).reshape(2, count, cap, width)
    v = swap(v.transpose(1, 0, 2, 3).reshape(rows, width), axis)
    v = v.reshape(count, 2, cap, width).transpose(1, 0, 2, 3).reshape(2, groups, GROUP, width)
    return v.transpose(1, 0, 2, 3).reshape(rows, width)


def from_behind(value, axis, steps):
    count = lax.axis_size(axis)
    pairs = [(source, (source + steps) % count) for source in range(count)]
    return lax.ppermute(value, axis, pairs)


def bias_tables(rel_bias):
    blocks, heads, entries = rel_bias.shape
    span = WIN * WIN
    pos = jnp.arange(span)
    half = WIN // 2
    row = (pos % (span // 2)) // half
    col = (pos // (span // 2)) * half + pos % half
    wide = 2 * WIN - 1
    index = (row[:, None] - row[None] + WIN - 1) * wide + col[:, None] - col[None] + WIN - 1
    onehot = (jnp.arange(entries)[:, None] == index.reshape(1, -1)).astype(BF16)
    rest = rel_bias.reshape(blocks * heads, entries)
    parts = []
    for _ in range(3):
        top = lax.reduce_precision(rest, 8, 7)
        parts.append(top)
        rest = rest - top
    stacked = jnp.concatenate(parts, axis=0).astype(BF16)
    got = jnp.dot(stacked, onehot, preferred_element_type=F32)
    got = got.reshape(3, blocks, heads, span, span)
    got = (got[0] + got[1]) + got[2]
    return got.transpose(0, 2, 1, 3).reshape(blocks, span, heads * span)


def body(
    bands, send_table, recv_table, regrid_weight, embed_weight, norm1_gain, qkv_weight, rel_bias,
    proj_weight, norm2_gain, up_weight, down_weight, unembed_weight,
):
    pd, width = bands.shape
    slots = send_table.shape[1]
    kk = recv_table.shape[0]
    d = embed_weight.shape[1]
    pixsq = regrid_weight.shape[1] // kk
    pix = int(round(pixsq**0.5))
    ch = width // pix
    half_cols = WIN // 2
    heads = rel_bias.shape[1]
    wide = pix * LANES
    ffh = up_weight.shape[2]
    groups = pd // GROUP

    outgoing = call(pick_kernel, [sds((slots, width), BF16)], [bands, send_table],
                    flops=2 * slots * pd * width, name="pick")
    incoming = swap(outgoing, "tile")

    recv = recv_table.reshape(kk, ROWS, 2, half_cols).transpose(0, 2, 1, 3).reshape(kk, pd)
    weight = regrid_weight.reshape(ROWS, 2, half_cols, kk * pixsq).transpose(1, 0, 2, 3)
    weight = weight.reshape(pd, kk * pixsq)
    gather, mix, wsend, select = call(
        prep_kernel,
        [sds((kk * pd, slots), BF16), sds((groups, pix * GROUP, kk * pix * GROUP), BF16),
         sds((kk * pd, pixsq), BF16), sds((kk * pd, pd), BF16)],
        [recv.reshape(kk * pd, 1), recv, weight], flops=2e9, name="prep")
    embed_pad = jnp.pad(embed_weight.reshape(pix, ch, d), ((0, 0), (0, LANES - ch), (0, 0)))
    embed_pad = embed_pad.reshape(wide, d)
    unembed_pad = jnp.pad(unembed_weight.reshape(d, pix, ch), ((0, 0), (0, 0), (0, LANES - ch)))
    unembed_pad = unembed_pad.reshape(d, wide)
    bias = bias_tables(rel_bias)

    wback = swap_pairs(wsend, "tile")

    vm = pltpu.VMEM
    half = pd // 2
    layer_scratch = [vm((d, 3 * d), BF16), vm((d, d), BF16), vm((d, ffh), BF16), vm((ffh, d), BF16)]
    low, high = call(
        first_kernel,
        [sds((half, d), BF16)] * 2,
        [incoming, gather, norm1_gain[:1], norm2_gain[:1], bias[0]],
        [mix, embed_pad, qkv_weight[0], proj_weight[0], up_weight[0], down_weight[0]],
        [vm((slots, wide), BF16), vm((kk, pd, wide), F32), vm((pd, wide), F32), vm(mix.shape, BF16),
         vm((wide, d), BF16), *layer_scratch, pltpu.SemaphoreType.DMA((6,))],
        flops=4e9, name="first")
    right = from_behind(low, "tile", -1)
    left = from_behind(high, "tile", 1)
    mix_back = call(prep_back_kernel, [sds((slots // GROUP, pix * GROUP, 2 * pix * GROUP), BF16)], [wback],
                    flops=2e9, name="prep_back")
    sent = call(
        second_kernel,
        [sds((kk * pd, d), BF16)],
        [low, high, left, right, norm1_gain[1:], norm2_gain[1:], bias[1]],
        [select, qkv_weight[1], proj_weight[1], up_weight[1], down_weight[1]],
        [vm((kk * pd, pd), BF16), *layer_scratch, pltpu.SemaphoreType.DMA((5,))],
        flops=2e9, name="second")
    got = swap_pairs(sent, "tile")
    return call(
        last_kernel,
        [sds((pd, width), F32)],
        [got, send_table, unembed_pad],
        [mix_back],
        [vm((kk * pd, wide), F32), vm((slots, wide), F32), vm(mix_back.shape, BF16),
         pltpu.SemaphoreType.DMA((1,))],
        flops=3e9, name="last")


def solution(mesh):
    in_specs = (
        P(("groups", "tile"), None), P("tile", None), P(None, "tile"), P("tile", None),
        P(), P(), P(), P(), P(), P(), P(), P(), P(),
    )
    out_specs = P(("groups", "tile"), None)
    return jax.shard_map(body, mesh=mesh, in_specs=in_specs, out_specs=out_specs, check_vma=False)
```

time: 159 us -> 110 us (0.69)
  matrix products: 38.7 us -> 0.77 us
  Pallas kernels: 0 us -> 30.8 us
  blocking collectives: 30.5 us -> 0 us
  other arithmetic: 19.9 us -> 0.16 us
  starting transfers between devices: 13.2 us -> 25 us
  local copies, waits for them, and re-layouts: 43 us -> 33.6 us
  waiting for transfers between devices: 11.9 us -> 18.4 us
    dot_general x15 -> x1, matrix products: 32.5 us -> 0.77 us  [bias_tables(): got = jnp.dot(stacked, onehot, preferred_element_type=F32)]
    pallas_call x0 -> x6, Pallas kernels: none -> 30.8 us  [call(): pl.pallas_call(kernel, out_shape=tuple(outs) if many else outs[0], in_spe...]
    all_to_all x1 -> x0, blocking collectives: 30.5 us -> none  [body(): lax.all_to_all(slot_sums.astype(jnp.bfloat16), 'tile', split_axis=0, conc...]
    reshape x11 -> x9, local copies, waits for them, and re-layouts: 26.9 us -> 4.95 us  [the longest x1 2.3 us: body(): embed_weight.reshape(pix, ch, d)]
    scatter-add x2 -> x0, other arithmetic: 17.5 us -> none  [the longest x1 12.1 us: body(): slot_sums = jnp.zeros((outgoing.shape[0], PIX * CH), jnp.float32).at[recv...]
    all_to_all x1 -> x3, waiting for transfers between devices: 3.85 us -> 17.2 us  [swap(): return lax.all_to_all(value, axis, split_axis=0, concat_axis=0, tiled=True)]
    all_to_all x1 -> x3, starting transfers between devices: 7.55 us -> 20.5 us  [swap(): return lax.all_to_all(value, axis, split_axis=0, concat_axis=0, tiled=True)]
    unnamed x25 -> x51, local copies, waits for them, and re-layouts: 2.82 us -> 14.9 us
  transfers between devices with their start and end apart: 3 -> 5, of which waited for: 3 -> 3; matrix products, arithmetic and copies ran while one was open for 13% -> 18% of each run, Pallas kernels for 0% -> 21%
where the time goes in v1:
time: 110 us; the launch traced here: 109 us
  local copies, waits for them, and re-layouts  33.6 us (31%)
  Pallas kernels  30.8 us (28%)
  starting transfers between devices  25 us (23%)
  waiting for transfers between devices  18.4 us (17%)
    pallas_call x6, Pallas kernels, call(): pl.pallas_call(kernel, out_shape=tuple(outs) if many else outs[0], in_spe...  30.8 us
    all_to_all x3, starting transfers between devices, swap(): return lax.all_to_all(value, axis, split_axis=0, concat_axis=0, tiled=True)  20.5 us
    all_to_all x3, waiting for transfers between devices, swap(): return lax.all_to_all(value, axis, split_axis=0, concat_axis=0, tiled=True)  17.2 us
    unnamed x51, local copies, waits for them, and re-layouts  14.9 us
    ppermute x2, starting transfers between devices, from_behind(): return lax.ppermute(value, axis, pairs)  4.49 us
    pad x1, local copies, waits for them, and re-layouts, body(): jnp.pad(embed_weight.reshape(pix, ch, d), ((0, 0), (0, LANES - ch), (0, 0)))  2.75 us
    reshape x1, local copies, waits for them, and re-layouts, body(): embed_weight.reshape(pix, ch, d)  2.3 us
  transfers between devices with their start and end apart: 5, of which 3 were waited for; matrix products, arithmetic and copies ran while one was open for 18% of the time, Pallas kernels for 21%

profile of v1, /device:TPU:0, one launch (start us, length us, event | category | flops | bytes accessed | tf_op | source)
XLA Modules:
  0.0 109.2 jit_solution(9250636521232107305)
XLA Ops:
  0.0 1.0 copy-done.3
  1.1 0.7 copy-done.8
  1.7 1.5 %pick.1 = bf16[384,1312]{1,0:T(8,128)(2,1)} custom-call(bf16[192,1312]{1,0:T(8,128)(2,1)S(1)} %copy-done.3, s32[1,384]{1,0:T(1,128)S(1)} %copy-done.8), custom_call_target="tpu_custom_call" | custom-call | flops 193462272 | bytes 1512960 | tf_op jit(solution)/shard_map/pick/pallas_call | solution.py:45
  3.2 7.6 %all-to-all-start = ((bf16[16,24,1312]{2,1,0:T(8,128)(2,1)}), bf16[16,24,1312]{2,1,0:T(8,128)(2,1)}, u32[]{:S(2)}, u32[]{:S(2)}) async-start(bf16[16,24,1312]{2,1,0:T(8,128)(2,1)} %bitcast), calls=%async_computation | async-start | bytes 2162688 | tf_op jit(solution)/shard_map/all_to_all | solution.py:356
  10.8 0.2 reshape.176
  11.3 0.1 reshape.178
  11.5 0.1 copy.29
  11.9 0.2 copy-done.23
  12.1 0.8 fusion
  12.9 0.3 add.111
  13.2 0.5 copy.28
  13.7 1.0 fusion.12
  14.8 0.2 copy-done.21
  15.0 0.9 slice_bitcast_fusion.6
  15.9 1.4 %prep.1 = (bf16[768,384]{1,0:T(8,128)(2,1)S(1)}, bf16[24,128,512]{2,1,0:T(8,128)(2,1)S(1)}, bf16[768,256]{1,0:T(8,128)(2,1)S(1)}, bf16[768,192]{1,0:T(8,128)(2,1)S(1)}) custom-call(s32[768,1]{1,0:T(8,128)S(1)} %reshape_reshape.4.recv_col_ref, s32[4,192]{1,0:T(4,128)S(1)} %reshape.177.recv_ref, bf16[192,1024]{1,0:T(8,128)(2,1)S(1)} %reshape.179.weight_ref), custom_call_target="tpu_custom_call" | custom-call | flops 2000000000 | bytes 4823040 | tf_op jit(solution)/shard_map/prep/pallas_call | solution.py:45
  17.4 0.7 copy-done.13
  18.1 0.8 copy-done.15
  18.9 1.4 %slice_bitcast_fusion.4 = (bf16[384,1152]{1,0:T(8,128)(2,1)}, bf16[384,1152]{1,0:T(8,128)(2,1)}) fusion(bf16[2,384,1152]{2,1,0:T(8,128)(2,1)S(1)} %copy-done.19), kind=kLoop, calls=%fused_computation.8 | loop fusion | bytes 3538944 | tf_op jit(solution)/shard_map/squeeze | solution.py:457
  20.3 1.2 %copy-done.12 = bf16[24,128,512]{2,1,0:T(8,128)(2,1)} copy-done((bf16[24,128,512]{2,1,0:T(8,128)(2,1)}, bf16[24,128,512]{2,1,0:T(8,128)(2,1)S(1)}, u32[]{:S(2)}) %copy-start.12) | copy-done | bytes 3145752
  21.5 0.8 copy-done.17
  22.3 0.2 slice_bitcast_fusion.1
  22.5 1.5 %copy-done.18 = bf16[2,1536,384]{2,1,0:T(8,128)(2,1)S(1)} copy-done((bf16[2,1536,384]{2,1,0:T(8,128)(2,1)S(1)}, bf16[2,1536,384]{2,1,0:T(8,128)(2,1)}, u32[]{:S(2)}) %copy-start.18) | copy-done | bytes 2359320
  24.0 1.3 %slice_bitcast_fusion = (bf16[1536,384]{1,0:T(8,128)(2,1)S(1)}, bf16[1536,384]{1,0:T(8,128)(2,1)}) fusion(bf16[2,1536,384]{2,1,0:T(8,128)(2,1)S(1)} %copy-done.18), kind=kLoop, calls=%fused_computation.3 | loop fusion | bytes 4718592 | tf_op jit(solution)/shard_map/squeeze | solution.py:457
  25.3 9.0 %all-to-all-done = bf16[16,24,1312]{2,1,0:T(8,128)(2,1)} async-done(((bf16[16,24,1312]{2,1,0:T(8,128)(2,1)}), bf16[16,24,1312]{2,1,0:T(8,128)(2,1)}, u32[]{:S(2)}, u32[]{:S(2)}) %all-to-all-start) | async-done | bytes 1007648 | tf_op jit(solution)/shard_map/all_to_all | solution.py:356
  34.3 7.0 %all-to-all-start.2 = ((bf16[16,48,256]{2,1,0:T(8,128)(2,1)}), bf16[16,48,256]{2,1,0:T(8,128)(2,1)}, u32[]{:S(2)}, u32[]{:S(2)}) async-start(bf16[16,48,256]{2,1,0:T(8,128)(2,1)} %bitcast.38), calls=%async_computation.2 | async-start | bytes 786432 | tf_op jit(solution)/shard_map/all_to_all | solution.py:356
  41.3 0.8 fusion.13
  42.1 1.9 %squeeze.33.bias_ref = f32[64,768]{1,0:T(8,128)} reshape(f32[1,64,12,64]{3,2,1,0:T(8,128)} %get-tuple-element.24) | data formatting | bytes 393216 | tf_op jit(solution)/shard_map/squeeze | solution.py:444
  43.9 2.3 %reshape.181 = bf16[16,82,384]{2,1,0:T(8,128)(2,1)} reshape(bf16[1312,384]{1,0:T(8,128)(2,1)} %param.17) | data formatting | bytes 2015232 | tf_op jit(solution)/shard_map/reshape | solution.py:430
  46.3 2.7 %pad.8 = bf16[16,128,384]{2,1,0:T(8,128)(2,1)} pad(bf16[16,82,384]{2,1,0:T(8,128)(2,1)} %reshape.181, bf16[]{:T(256)} %constant.72.clone.1), padding=0_0x0_46x0_0 | pad | bytes 2580482 | tf_op jit(solution)/shard_map/jit(_pad)/pad | solution.py:430
  49.0 1.1 copy-done.16
  50.1 11.2 %first.1 = (bf16[96,384]{1,0:T(8,128)(2,1)}, bf16[96,384]{1,0:T(8,128)(2,1)}) custom-call(bf16[384,1312]{1,0:T(8,128)(2,1)} %bitcast.1.inc_ref, bf16[768,384]{1,0:T(8,128)(2,1)S(1)} %copy-done.16, f32[1,384]{1,0:T(1,128)S(1)} %get-tuple-element.36.gain1_ref, f32[1,384]{1,0:T(1,128)S(1)} %get-tuple-element.31.gain2_ref, f32[64,768]{1,0:T(8,128)S(1)} %copy-done.7, ...), custom_call_target="tpu_custom_call" | custom-call | flops 4000000000 | bytes 10202112 | tf_op jit(solution)/shard_map/first/pallas_call | solution.py:45
  61.3 0.4 collective-permute-start
  61.7 4.1 %collective-permute-start.1 = (bf16[96,384]{1,0:T(8,128)(2,1)}, bf16[96,384]{1,0:T(8,128)(2,1)S(1)}, u32[]{:S(2)}, u32[]{:S(2)}) collective-permute-start(bf16[96,384]{1,0:T(8,128)(2,1)} %get-tuple-element.13.low_ref), channel_id=1, source_target_pairs={{0,15},{1,0},{2,1},{3,2},{4,3},{5,4},{6,5},{7,6},{8,7},{9,8},{10,9... | collective-permute-start | bytes 221192 | tf_op jit(solution)/shard_map/ppermute | solution.py:375
  65.8 1.2 %squeeze.38.bias_ref = f32[64,768]{1,0:T(8,128)S(1)} reshape(f32[1,64,12,64]{3,2,1,0:T(8,128)} %get-tuple-element.23) | data formatting | bytes 393216 | tf_op jit(solution)/shard_map/squeeze | solution.py:456
  67.0 1.2 %collective-permute-done.left_ref = bf16[96,384]{1,0:T(8,128)(2,1)S(1)} collective-permute-done((bf16[96,384]{1,0:T(8,128)(2,1)}, bf16[96,384]{1,0:T(8,128)(2,1)S(1)}, u32[]{:S(2)}, u32[]{:S(2)}) %collective-permute-start) | collective-permute-done | bytes 73760 | tf_op jit(solution)/shard_map/ppermute | solution.py:375
  68.1 1.2 %copy-done.1 = bf16[384,1152]{1,0:T(8,128)(2,1)S(1)} copy-done((bf16[384,1152]{1,0:T(8,128)(2,1)S(1)}, bf16[384,1152]{1,0:T(8,128)(2,1)}, u32[]{:S(2)}) %copy-start.1) | copy-done | bytes 884760
  69.3 1.0 copy-done.5
  70.3 1.0 copy-done.14
  71.3 8.2 %second.1 = bf16[768,384]{1,0:T(8,128)(2,1)} custom-call(bf16[96,384]{1,0:T(8,128)(2,1)} %get-tuple-element.13.low_ref, bf16[96,384]{1,0:T(8,128)(2,1)} %get-tuple-element.14.high_ref, bf16[96,384]{1,0:T(8,128)(2,1)S(1)} %collective-permute-done.left_ref, bf16[96,384]{1,0:T(8,128)(2,1)S(1)} %collective-permute-done.1.right_ref, ...), custom_call_target="tpu_custom_call" | custom-call | flops 2000000000 | bytes 4918272 | tf_op jit(solution)/shard_map/second/pallas_call | solution.py:45
  79.5 5.9 %all-to-all-start.1 = ((bf16[16,48,384]{2,1,0:T(8,128)(2,1)}), bf16[16,48,384]{2,1,0:T(8,128)(2,1)S(1)}, u32[]{:S(2)}, u32[]{:S(2)}) async-start(bf16[16,48,384]{2,1,0:T(8,128)(2,1)} %bitcast.14), calls=%async_computation.1 | async-start | bytes 1179648 | tf_op jit(solution)/shard_map/all_to_all | solution.py:356
  85.4 0.3 reshape.183
  85.7 1.4 %pad.9 = bf16[384,16,128]{0,2,1:T(8,128)(2,1)} pad(bf16[384,16,82]{0,2,1:T(8,128)(2,1)S(1)} %reshape.183, bf16[]{:T(256)} %constant.72.clone.1), padding=0_0x0_0x0_46 | pad | bytes 2580482 | tf_op jit(solution)/shard_map/jit(_pad)/pad | solution.py:432
  87.1 1.7 %copy.25.unembed_ref = bf16[384,2048]{1,0:T(8,128)(2,1)S(1)} copy(bf16[384,2048]{0,1:T(8,128)(2,1)} %bitcast.39) | data formatting | bytes 3145728 | tf_op jit(solution)/shard_map/reshape | solution.py:433
  88.8 2.1 %prep_back.1.mix_any = bf16[48,128,256]{2,1,0:T(8,128)(2,1)S(1)} custom-call(bf16[768,256]{1,0:T(8,128)(2,1)} %bitcast.18.weight_ref), custom_call_target="tpu_custom_call" | custom-call | flops 2000000000 | bytes 3538944 | tf_op jit(solution)/shard_map/prep_back/pallas_call | solution.py:45
  90.9 1.6 %copy-done.10 = bf16[48,128,256]{2,1,0:T(8,128)(2,1)} copy-done((bf16[48,128,256]{2,1,0:T(8,128)(2,1)}, bf16[48,128,256]{2,1,0:T(8,128)(2,1)S(1)}, u32[]{:S(2)}) %copy-start.10) | copy-done | bytes 3145752
  92.6 8.2 %all-to-all-done.1 = bf16[16,48,384]{2,1,0:T(8,128)(2,1)S(1)} async-done(((bf16[16,48,384]{2,1,0:T(8,128)(2,1)}), bf16[16,48,384]{2,1,0:T(8,128)(2,1)S(1)}, u32[]{:S(2)}, u32[]{:S(2)}) %all-to-all-start.1) | async-done | bytes 589856 | tf_op jit(solution)/shard_map/all_to_all | solution.py:356
  100.8 1.9 %copy-done.11 = bf16[48,128,256]{2,1,0:T(8,128)(2,1)S(1)} copy-done((bf16[48,128,256]{2,1,0:T(8,128)(2,1)S(1)}, bf16[48,128,256]{2,1,0:T(8,128)(2,1)}, u32[]{:S(2)}) %copy-start.11) | copy-done | bytes 3145752
  102.6 6.4 %last.1 = f32[192,1312]{1,0:T(8,128)} custom-call(bf16[768,384]{1,0:T(8,128)(2,1)S(1)} %bitcast.37, s32[1,384]{1,0:T(1,128)S(1)} %copy-done.9, bf16[384,2048]{1,0:T(8,128)(2,1)S(1)} %copy.25.unembed_ref, bf16[48,128,256]{2,1,0:T(8,128)(2,1)S(1)} %copy-done.11), custom_call_target="tpu_custom_call" | custom-call | flops 3000000000 | bytes 6317568 | tf_op jit(solution)/shard_map/last/pallas_call | solution.py:45
  (48 shorter events, 0.7 us)
Async XLA Ops:
  0.0 1.0 copy-start.3
  1.0 0.7 copy-start.8
  3.2 7.6 %copy-start.24 = (s32[4,192]{1,0:T(4,128)S(1)}, s32[4,192]{1,0:T(4,128)}, u32[]{:S(2)}) copy-start(s32[4,192]{1,0:T(4,128)} %param.15) | copy-start | bytes 9220
  3.2 8.1 %copy-start.22 = (bf16[192,1024]{1,0:T(8,128)(2,1)S(1)}, bf16[192,1024]{1,0:T(8,128)(2,1)}, u32[]{:S(2)}) copy-start(bf16[192,1024]{1,0:T(8,128)(2,1)} %param.16) | copy-start | bytes 1179652
  3.2 31.1 %all-to-all-start = ((bf16[16,24,1312]{2,1,0:T(8,128)(2,1)}), bf16[16,24,1312]{2,1,0:T(8,128)(2,1)}, u32[]{:S(2)}, u32[]{:S(2)}) async-start(bf16[16,24,1312]{2,1,0:T(8,128)(2,1)} %bitcast), calls=%async_computation | async-start | bytes 2162688 | tf_op jit(solution)/shard_map/all_to_all | solution.py:356
  11.3 0.7 copy-start.23
  13.7 1.3 %copy-start.21 = (bf16[2,384,384]{2,1,0:T(8,128)(2,1)S(1)}, bf16[2,384,384]{2,1,0:T(8,128)(2,1)}, u32[]{:S(2)}) copy-start(bf16[2,384,384]{2,1,0:T(8,128)(2,1)} %param.21) | copy-start | bytes 1769476
  15.9 3.0 %copy-start.19 = (bf16[2,384,1152]{2,1,0:T(8,128)(2,1)S(1)}, bf16[2,384,1152]{2,1,0:T(8,128)(2,1)}, u32[]{:S(2)}) copy-start(bf16[2,384,1152]{2,1,0:T(8,128)(2,1)} %param.19) | copy-start | bytes 5308420
  17.3 0.8 copy-start.13
  18.1 0.8 copy-start.15
  18.9 1.4 %copy-start.4 = (bf16[768,256]{1,0:T(8,128)(2,1)}, bf16[768,256]{1,0:T(8,128)(2,1)S(1)}, u32[]{:S(2)}) copy-start(bf16[768,256]{1,0:T(8,128)(2,1)S(1)} %get-tuple-element.16) | copy-start | bytes 1179652
  18.9 2.6 %copy-start.12 = (bf16[24,128,512]{2,1,0:T(8,128)(2,1)}, bf16[24,128,512]{2,1,0:T(8,128)(2,1)S(1)}, u32[]{:S(2)}) copy-start(bf16[24,128,512]{2,1,0:T(8,128)(2,1)S(1)} %get-tuple-element.12.mix_any) | copy-start | bytes 9437188
  18.9 3.4 %copy-start.17 = (bf16[2,384,1536]{2,1,0:T(8,128)(2,1)S(1)}, bf16[2,384,1536]{2,1,0:T(8,128)(2,1)}, u32[]{:S(2)}) copy-start(bf16[2,384,1536]{2,1,0:T(8,128)(2,1)} %param.23) | copy-start | bytes 7077892
  22.3 1.7 %copy-start.18 = (bf16[2,1536,384]{2,1,0:T(8,128)(2,1)S(1)}, bf16[2,1536,384]{2,1,0:T(8,128)(2,1)}, u32[]{:S(2)}) copy-start(bf16[2,1536,384]{2,1,0:T(8,128)(2,1)} %param.24) | copy-start | bytes 7077892
  34.3 45.2 %all-to-all-start.2 = ((bf16[16,48,256]{2,1,0:T(8,128)(2,1)}), bf16[16,48,256]{2,1,0:T(8,128)(2,1)}, u32[]{:S(2)}, u32[]{:S(2)}) async-start(bf16[16,48,256]{2,1,0:T(8,128)(2,1)} %bitcast.38), calls=%async_computation.2 | async-start | bytes 786432 | tf_op jit(solution)/shard_map/all_to_all | solution.py:356
  46.2 2.8 %copy-start = (bf16[1536,384]{1,0:T(8,128)(2,1)S(1)}, bf16[1536,384]{1,0:T(8,128)(2,1)}, u32[]{:S(2)}) copy-start(bf16[1536,384]{1,0:T(8,128)(2,1)} %get-tuple-element.18.down_any) | copy-start | bytes 3538948
  46.2 2.8 %copy-start.2 = (bf16[384,1152]{1,0:T(8,128)(2,1)S(1)}, bf16[384,1152]{1,0:T(8,128)(2,1)}, u32[]{:S(2)}) copy-start(bf16[384,1152]{1,0:T(8,128)(2,1)} %get-tuple-element.22.qkv_any) | copy-start | bytes 2654212
  46.2 2.8 %copy-start.6 = (bf16[384,384]{1,0:T(8,128)(2,1)S(1)}, bf16[384,384]{1,0:T(8,128)(2,1)}, u32[]{:S(2)}) copy-start(bf16[384,384]{1,0:T(8,128)(2,1)} %get-tuple-element.26.proj_any) | copy-start | bytes 884740
  46.2 2.8 %copy-start.7 = (f32[64,768]{1,0:T(8,128)S(1)}, f32[64,768]{1,0:T(8,128)}, u32[]{:S(2)}) copy-start(f32[64,768]{1,0:T(8,128)} %squeeze.33.bias_ref) | copy-start | bytes 589828
  49.0 1.1 copy-start.16
  61.3 6.8 %collective-permute-start = (bf16[96,384]{1,0:T(8,128)(2,1)}, bf16[96,384]{1,0:T(8,128)(2,1)S(1)}, u32[]{:S(2)}, u32[]{:S(2)}) collective-permute-start(bf16[96,384]{1,0:T(8,128)(2,1)} %get-tuple-element.14.high_ref), channel_id=1, source_target_pairs={{0,1},{1,2},{2,3},{3,4},{4,5},{5,6},{6,7},{7,8},{8,9},{9,10},{10,1... | collective-permute-start | bytes 221192 | tf_op jit(solution)/shard_map/ppermute | solution.py:375
  61.7 6.4 %collective-permute-start.1 = (bf16[96,384]{1,0:T(8,128)(2,1)}, bf16[96,384]{1,0:T(8,128)(2,1)S(1)}, u32[]{:S(2)}, u32[]{:S(2)}) collective-permute-start(bf16[96,384]{1,0:T(8,128)(2,1)} %get-tuple-element.13.low_ref), channel_id=1, source_target_pairs={{0,15},{1,0},{2,1},{3,2},{4,3},{5,4},{6,5},{7,6},{8,7},{9,8},{10,9... | collective-permute-start | bytes 221192 | tf_op jit(solution)/shard_map/ppermute | solution.py:375
  68.1 1.2 %copy-start.1 = (bf16[384,1152]{1,0:T(8,128)(2,1)S(1)}, bf16[384,1152]{1,0:T(8,128)(2,1)}, u32[]{:S(2)}) copy-start(bf16[384,1152]{1,0:T(8,128)(2,1)} %get-tuple-element.21.qkv_any) | copy-start | bytes 2654212
  69.3 1.0 copy-start.5
  70.3 1.0 copy-start.14
  79.5 5.9 %copy-start.20 = (bf16[384,1312]{0,1:T(8,128)(2,1)S(1)}, bf16[384,1312]{0,1:T(8,128)(2,1)}, u32[]{:S(2)}) copy-start(bf16[384,1312]{0,1:T(8,128)(2,1)} %param.25) | copy-start | bytes 3022852
  79.5 21.2 %all-to-all-start.1 = ((bf16[16,48,384]{2,1,0:T(8,128)(2,1)}), bf16[16,48,384]{2,1,0:T(8,128)(2,1)S(1)}, u32[]{:S(2)}, u32[]{:S(2)}) async-start(bf16[16,48,384]{2,1,0:T(8,128)(2,1)} %bitcast.14), calls=%async_computation.1 | async-start | bytes 1179648 | tf_op jit(solution)/shard_map/all_to_all | solution.py:356
  88.8 12.0 %copy-start.9 = (s32[1,384]{1,0:T(1,128)S(1)}, s32[1,384]{1,0:T(1,128)}, u32[]{:S(2)}) copy-start(s32[1,384]{1,0:T(1,128)} %send_ref.3) | copy-start | bytes 4612
  90.9 1.6 %copy-start.10 = (bf16[48,128,256]{2,1,0:T(8,128)(2,1)}, bf16[48,128,256]{2,1,0:T(8,128)(2,1)S(1)}, u32[]{:S(2)}) copy-start(bf16[48,128,256]{2,1,0:T(8,128)(2,1)S(1)} %prep_back.1.mix_any) | copy-start | bytes 9437188
  100.8 1.9 %copy-start.11 = (bf16[48,128,256]{2,1,0:T(8,128)(2,1)S(1)}, bf16[48,128,256]{2,1,0:T(8,128)(2,1)}, u32[]{:S(2)}) copy-start(bf16[48,128,256]{2,1,0:T(8,128)(2,1)} %copy-done.10) | copy-start | bytes 9437188
